TPU v7x, 256 devices: a whole 4x4x8 slice. The times are simulated.
256 devices in a mesh: outer: 16 (over y, x), inner: 16 (over z, core).
Axes of the slice: x: 4, y: 4, z: 8, core: 2. Of those that a mesh axis runs over, the one named last changes fastest.
Arguments:
- tokens: bfloat16 [65536, 8192], P(('outer', 'inner')), may hold values from -24 to 24
- upstream: bfloat16 [65536, 8192], P(('outer', 'inner')), may hold values from -24 to 24
- weights: bfloat16 [3, 8192, 256], P(None, ('outer', 'inner')), may hold values from -0.0625 to 0.0625
Outputs:
- gradients: float32 [3, 256, 8192], P(None, 'inner', 'outer')
All inputs are finite; a program needn't handle non-finite values.
Results may differ from a plain program's by a relative error of at most 0.0049.
Values may be sent and summed in bfloat16 or wider, within the bound.
A program may use at most 128 MiB of HBM per device.

v0:
```python
import jax
import jax.numpy as jnp
from jax import lax
from jax.sharding import PartitionSpec as P


def cut_along(value, dim, size):
    before, after = (value.shape[:dim], value.shape[dim + 1 :])
    return jnp.moveaxis(value.reshape(*before, size, -1, *after), dim, 0)


def piece_ends(length, count):
    step = length // count
    if step >= 8:
        step -= step % 8
    return [step * k for k in range(1, count)]


def in_order(tiles, dim):
    tiles = jnp.moveaxis(tiles, 0, dim)
    shape = tiles.shape
    return tiles.reshape(*shape[:dim], shape[dim] * shape[dim + 1], *shape[dim + 2 :])


def exchange_in_pieces(value, axis, pieces, split_dim, concat_dim):
    tiles = cut_along(value, split_dim, lax.axis_size(axis))
    cut = max(range(1, max(2, tiles.ndim - 1)), key=lambda d: tiles.shape[d])
    done = []
    for share in jnp.split(tiles, piece_ends(tiles.shape[cut], pieces), axis=cut):
        if share.size:
            done.append(lax.all_to_all(share, axis, split_axis=0, concat_axis=0, tiled=True))
    return in_order(jnp.concatenate(done, axis=cut), concat_dim)


def combine_received(received):
    return jnp.sum(received.astype(jnp.float32), axis=0)


def on_device(tokens, upstream, weights):
    full_weights = lax.all_gather(weights, ("outer", "inner"), axis=1, tiled=True)
    gate_pre = jnp.dot(tokens, full_weights[0], preferred_element_type=jnp.float32)
    up_pre = jnp.dot(tokens, full_weights[1], preferred_element_type=jnp.float32)
    hidden_grad = jnp.dot(upstream, full_weights[2], preferred_element_type=jnp.float32)
    sigmoid = jax.nn.sigmoid(gate_pre)
    activated = gate_pre * sigmoid
    hidden = (activated * up_pre).astype(jnp.bfloat16)
    grad_gate = (hidden_grad * up_pre * sigmoid * (1.0 + gate_pre * (1.0 - sigmoid))).astype(
        jnp.bfloat16
    )
    grad_up = (hidden_grad * activated).astype(jnp.bfloat16)
    stacked = jnp.stack(
        [
            jnp.dot(grad_gate.T, tokens, preferred_element_type=jnp.float32),
            jnp.dot(grad_up.T, tokens, preferred_element_type=jnp.float32),
            jnp.dot(hidden.T, upstream, preferred_element_type=jnp.float32),
        ]
    ).astype(jnp.bfloat16)
    received = exchange_in_pieces(stacked[None], "inner", 2, 2, 0)
    partial_sum = combine_received(received)
    partial_rounded = partial_sum.astype(jnp.bfloat16)
    final_pieces = lax.all_to_all(
        partial_rounded[None], "outer", split_axis=3, concat_axis=0, tiled=True
    )
    return combine_received(final_pieces)


def solution(mesh):
    placed = (
        P(("outer", "inner"), None),
        P(("outer", "inner"), None),
        P(None, ("outer", "inner"), None),
    )
    return jax.shard_map(
        on_device, mesh=mesh, in_specs=placed, out_specs=P(None, "inner", "outer"), check_vma=False
    )
```

profile of v0, /device:TPU:1, one launch (start us, length us, event | category | flops | bytes accessed | tf_op | source)
XLA Modules:
  0.0 518.0 jit_solution(4578464147569142469)
XLA Ops:
  6.5 0.0 all-gather.2.cloned.1.call-start
  6.5 0.7 all-gather.2.cloned.1.call-update
  7.3 129.5 %all-gather.2.cloned.1.call-done = bf16[3,8192,256]{2,1,0:T(8,128)(2,1)} async-done(((bf16[3,32,256]{2,1,0:T(8,128)(2,1)}), bf16[3,8192,256]{2,1,0:T(8,128)(2,1)}) %all-gather.2.cloned.1.call-update) | async-done | bytes 12582928 | tf_op jit(solution)/shard_map/all_gather | solution.py:40
  136.8 0.0 copy-start.1
  136.8 4.8 fusion
  141.6 0.0 copy-done.1
  141.6 0.0 copy-start
  141.6 3.6 fusion.2
  145.2 0.0 copy-done
  145.2 1.3 convolution_convert_fusion.1
  146.5 3.4 fusion.1
  150.0 1.3 convolution_convert_fusion.2
  151.3 1.3 convolution_convert_fusion
  152.6 1.6 maximum_bitcast_fusion
  154.3 1.3 fusion.10
  155.6 145.4 %all_to_all.19 = bf16[16,1,3,8,8192]{4,3,2,1,0:T(8,128)(2,1)} all-to-all(bf16[16,1,3,8,8192]{4,3,2,1,0:T(8,128)(2,1)S(1)} %get-tuple-element.5), channel_id=1, replica_groups=mesh['outer'=16,'inner'=16] {'inner'}, dimensions={0} | all-to-all | bytes 12582912 | tf_op jit(solution)/shard_map/all_to_all | solution.py:31
  301.0 143.6 %all_to_all.20 = bf16[16,1,3,8,8192]{4,3,2,1,0:T(8,128)(2,1)} all-to-all(bf16[16,1,3,8,8192]{4,3,2,1,0:T(8,128)(2,1)S(1)} %get-tuple-element.6), channel_id=1, replica_groups=mesh['outer'=16,'inner'=16] {'inner'}, dimensions={0} | all-to-all | bytes 12582912 | tf_op jit(solution)/shard_map/all_to_all | solution.py:31
  444.7 6.6 %maximum_reduce_fusion = bf16[3,16,8192]{2,1,0:T(8,128)(2,1)S(1)} fusion(bf16[16,1,3,8,8192]{4,3,2,1,0:T(8,128)(2,1)} %all_to_all.20, bf16[16,1,3,8,8192]{4,3,2,1,0:T(8,128)(2,1)} %all_to_all.19), kind=kLoop, calls=%fused_computation.2 | loop fusion | flops 31064064 | bytes 13369344 | tf_op jit(solution)/shard_map/reduce_sum | solution.py:36
  451.3 8.3 %copy.10 = bf16[1,3,16,8192]{2,1,0,3:T(4,128)(2,1)} copy(bf16[1,3,16,8192]{3,2,1,0:T(8,128)(2,1)S(1)} %bitcast.36) | data formatting | bytes 1572864 | tf_op jit(solution)/shard_map/broadcast_in_dim | solution.py:62
  459.6 12.8 %reshape.54 = bf16[16,2,12288]{2,1,0:T(2,128)(2,1)S(1)} reshape(bf16[8192,1,3,16]{3,2,1,0:T(4,128)(2,1)} %bitcast.31) | data formatting | bytes 1572864
  472.4 18.9 %all_to_all.21 = bf16[16,2,12288]{2,1,0:T(2,128)(2,1)S(1)} all-to-all(bf16[16,2,12288]{2,1,0:T(2,128)(2,1)S(1)} %reshape.54), channel_id=1, replica_groups=mesh['outer'=16,'inner'=16] {'outer'}, dimensions={0} | all-to-all | bytes 1572864 | tf_op jit(solution)/shard_map/all_to_all | solution.py:61
  491.3 10.7 %reshape.55 = bf16[8192,1,3,16]{3,2,1,0:T(4,128)(2,1)} reshape(bf16[16,2,12288]{2,1,0:T(2,128)(2,1)S(1)} %all_to_all.21) | data formatting | bytes 1572864
  502.1 8.1 %convert_reduce_fusion = f32[3,16,512]{1,0,2:T(4,128)S(1)} fusion(bf16[3,16,16,512]{1,0,3,2:T(4,128)(2,1)} %bitcast.32), kind=kLoop, calls=%fused_computation | loop fusion | flops 761856 | bytes 884736 | tf_op jit(solution)/shard_map/reduce_sum | solution.py:36
  510.2 0.9 copy.11
Async XLA Ops:
  6.5 130.2 %all-gather.2.cloned.1.call-start = ((), (), s32[]{:S(2)}) async-start(), calls=%async_computation.3 | async-start | bytes 12632064 | tf_op jit(solution)/shard_map/all_gather | solution.py:40
  136.8 4.9 copy-start.1
  141.6 3.6 copy-start
Sparse Core Ops, SparseCore 0:
  11.0 125.7 all-gather.1
where the time goes:
time: 518 us
  blocking collectives  308 us (59%)
  waiting for transfers between devices  130 us (25%)
  local copies, waits for them, and re-layouts  34.1 us (7%)
  other arithmetic  16.4 us (3%)
  matrix products  15.8 us (3%)
  between operations  13.5 us (3%)
    all_to_all x2, blocking collectives, exchange_in_pieces(): lax.all_to_all(share, axis, split_axis=0, concat_axis=0, tiled=True)  289 us
    all_gather x1, waiting for transfers between devices, on_device(): lax.all_gather(weights, ('outer', 'inner'), axis=1, tiled=True)  129 us
    unnamed x6, local copies, waits for them, and re-layouts  23.6 us
    all_to_all x1, blocking collectives, on_device(): lax.all_to_all(partial_rounded[None], 'outer', split_axis=3, concat_axis=...  18.9 us
    reduce_sum x2, other arithmetic, combine_received(): return jnp.sum(received.astype(jnp.float32), axis=0)  14.8 us
  transfers between devices with their start and end apart: 1, of which 1 were waited for; matrix products, arithmetic and copies ran while one was open for 0% of the time, Pallas kernels for 0%

commit v1 on v0

--- a/solution.py
+++ b/solution.py
@@ -58,8 +58,14 @@
     received = exchange_in_pieces(stacked[None], "inner", 2, 2, 0)
     partial_sum = combine_received(received)
     partial_rounded = partial_sum.astype(jnp.bfloat16)
-    final_pieces = lax.all_to_all(
-        partial_rounded[None], "outer", split_axis=3, concat_axis=0, tiled=True
+    final_pieces = jnp.concatenate(
+        lax.all_to_all(
+            jnp.stack(jnp.split(partial_rounded[None], lax.axis_size("outer"), axis=3)),
+            "outer",
+            0,
+            0,
+        ),
+        axis=0,
     )
     return combine_received(final_pieces)
 

time: 518 us -> 478 us (0.923)
  local copies, waits for them, and re-layouts: 34.1 us -> 1.44 us
  other arithmetic: 16.4 us -> 9 us
    unnamed x6 -> x19, local copies, waits for them, and re-layouts: 23.6 us -> 0.1 us
    broadcast_in_dim x1 -> x0, local copies, waits for them, and re-layouts: 8.27 us -> none  [on_device(): partial_rounded[None]]
    reduce_sum x2, other arithmetic: 14.8 us -> 7.39 us  [combine_received(): return jnp.sum(received.astype(jnp.float32), axis=0)]
where the time goes in v1:
time: 478 us
  blocking collectives  308 us (64%)
  waiting for transfers between devices  130 us (27%)
  matrix products  15.8 us (3%)
  between operations  13.6 us (3%)
  other arithmetic  9 us (2%)
    all_to_all x2, blocking collectives, exchange_in_pieces(): lax.all_to_all(share, axis, split_axis=0, concat_axis=0, tiled=True)  289 us
    all_gather x1, waiting for transfers between devices, on_device(): lax.all_gather(weights, ('outer', 'inner'), axis=1, tiled=True)  129 us
    all_to_all x1, blocking collectives, on_device(): lax.all_to_all(jnp.stack(jnp.split(partial_rounded[None], lax.axis_size('...  18.9 us
  transfers between devices with their start and end apart: 1, of which 1 were waited for; matrix products, arithmetic and copies ran while one was open for 0% of the time, Pallas kernels for 0%

profile of v1, /device:TPU:1, one launch (start us, length us, event | category | flops | bytes accessed | tf_op | source)
XLA Modules:
  0.0 478.1 jit_solution(1224984278567526773)
XLA Ops:
  6.5 0.0 all-gather.2.cloned.1.call-start
  6.5 0.7 all-gather.2.cloned.1.call-update
  7.3 129.5 %all-gather.2.cloned.1.call-done = bf16[3,8192,256]{2,1,0:T(8,128)(2,1)} async-done(((bf16[3,32,256]{2,1,0:T(8,128)(2,1)}), bf16[3,8192,256]{2,1,0:T(8,128)(2,1)}) %all-gather.2.cloned.1.call-update) | async-done | bytes 12582928 | tf_op jit(solution)/shard_map/all_gather | solution.py:40
  136.8 0.0 copy-start.1
  136.8 4.8 %fusion = f32[256,256]{1,0:T(8,128)S(1)} fusion(bf16[256,8192]{1,0:T(8,128)(2,1)} %param.3, bf16[3,8192,256]{2,1,0:T(8,128)(2,1)} %all-gather.2.cloned.1.call-done), kind=kOutput, calls=%fused_computation.6 | convolution fusion | flops 1073741824 | bytes 8650752 | tf_op jit(solution)/shard_map/dot_general | solution.py:41
  141.6 0.0 copy-done.1
  141.6 0.0 copy-start
  141.6 3.6 fusion.2
  145.2 0.0 copy-done
  145.2 1.3 convolution_convert_fusion.1
  146.5 3.4 fusion.1
  150.0 1.3 convolution_convert_fusion.2
  151.3 1.3 convolution_convert_fusion
  152.7 1.6 maximum_bitcast_fusion
  154.3 1.3 fusion.26
  155.6 145.4 %all_to_all.15 = bf16[16,1,3,8,8192]{4,3,2,1,0:T(8,128)(2,1)} all-to-all(bf16[16,1,3,8,8192]{4,3,2,1,0:T(8,128)(2,1)S(1)} %get-tuple-element.5), channel_id=1, replica_groups=mesh['outer'=16,'inner'=16] {'inner'}, dimensions={0} | all-to-all | bytes 12582912 | tf_op jit(solution)/shard_map/all_to_all | solution.py:31
  301.0 143.6 %all_to_all.16 = bf16[16,1,3,8,8192]{4,3,2,1,0:T(8,128)(2,1)} all-to-all(bf16[16,1,3,8,8192]{4,3,2,1,0:T(8,128)(2,1)S(1)} %get-tuple-element.6), channel_id=1, replica_groups=mesh['outer'=16,'inner'=16] {'inner'}, dimensions={0} | all-to-all | bytes 12582912 | tf_op jit(solution)/shard_map/all_to_all | solution.py:31
  444.7 6.6 %maximum_reduce_fusion = bf16[3,16,8192]{2,1,0:T(8,128)(2,1)S(1)} fusion(bf16[16,1,3,8,8192]{4,3,2,1,0:T(8,128)(2,1)} %all_to_all.16, bf16[16,1,3,8,8192]{4,3,2,1,0:T(8,128)(2,1)} %all_to_all.15), kind=kLoop, calls=%fused_computation.1 | loop fusion | flops 31064064 | bytes 13369344 | tf_op jit(solution)/shard_map/reduce_sum | solution.py:36
  451.5 18.9 %all_to_all.17 = bf16[16,1,3,16,512]{4,3,2,1,0:T(8,128)(2,1)S(1)} all-to-all(bf16[16,1,3,16,512]{4,3,2,1,0:T(8,128)(2,1)S(1)} %fusion.5), channel_id=1, replica_groups=mesh['outer'=16,'inner'=16] {'outer'}, dimensions={0} | all-to-all | bytes 1572864 | tf_op jit(solution)/shard_map/all_to_all | solution.py:62
  470.4 0.8 convert_reduce_fusion
  (16 shorter events, 0.1 us)
Async XLA Ops:
  6.5 130.2 %all-gather.2.cloned.1.call-start = ((), (), s32[]{:S(2)}) async-start(), calls=%async_computation.3 | async-start | bytes 12632064 | tf_op jit(solution)/shard_map/all_gather | solution.py:40
  136.8 4.9 %copy-start.1 = (bf16[256,8192]{1,0:T(8,128)(2,1)S(1)}, bf16[256,8192]{1,0:T(8,128)(2,1)}, u32[]{:S(2)}) copy-start(bf16[256,8192]{1,0:T(8,128)(2,1)} %param.4) | copy-start | bytes 12582916
  141.6 3.6 copy-start
Sparse Core Ops, SparseCore 0:
  11.0 125.7 all-gather.1
